TPU v7x, 512 devices: a whole 4x4x16 slice. The times are simulated.
512 devices in a mesh: snode: 128 (over z, x, core), rhs: 4 (over y).
Axes of the slice: x: 4, y: 4, z: 16, core: 2. Of those that a mesh axis runs over, the one named last changes fastest.
Arguments:
- right_sides: float32 [3, 256, 256, 512], P(None, 'snode', None, 'rhs'), may hold values from -6 to 6
- diag_inverse: float32 [3, 256, 256, 256], P(None, 'snode', 'rhs')
- off_diagonal: bfloat16 [2, 256, 1024, 256], P(None, 'snode'), may hold values from -0.125 to 0.125
- target_snode: int32 [2, 256, 64], P(None, 'snode'), may hold values from 0 to 255, as said below
- target_block: int32 [2, 256, 64], P(None, 'snode'), may hold values from 0 to 15
Outputs:
- solution: float32 [3, 256, 256, 512], P(None, 'snode', None, 'rhs')
Inputs may be any that keep to these rules, and one draw needn't show every extreme that they name: `target_snode`: each entry is a supernode's position in the next level; the supernodes at positions i * 2 to i * 2 + 1 belong to index i of snode. Of one level's blocks held by one index of snode, at most 2 name supernodes of any one index, and some index receives exactly 2 from every index in every level.
All inputs are finite; a program needn't handle non-finite values.
Results may differ from a plain program's by a relative error of at most 0.0038.
Values may be sent and summed in bfloat16 or wider, within the bound.
No kernel may reach another device: no remote copies, remote signals or barrier semaphores. Data moves between devices by JAX's collectives and lax.ppermute only.
A program may use at most 64 MiB of HBM per device.

v0:
```python
import jax
import jax.numpy as jnp
from jax import lax
from jax.sharding import PartitionSpec as P

BR = 16


def on_device(right_sides, diag_inverse, off_diagonal, target_snode, target_block):
    precise = lax.Precision.HIGHEST
    levels = right_sides.shape[0]
    local_nodes = right_sides.shape[1]
    order_size = right_sides.shape[2]
    columns = right_sides.shape[3]
    per_node = target_snode.shape[2]
    row_blocks = order_size // BR
    devices = lax.axis_size("snode")
    outgoing = local_nodes * per_node
    capacity = 2 * outgoing // devices
    slot_count = devices * capacity
    local_rows = local_nodes * row_blocks
    front_count = 1
    front_width = columns // front_count
    full_diag = [
        lax.all_gather(diag_inverse[height], "rhs", axis=1, tiled=True) for height in range(levels)
    ]
    block_order = lax.iota(jnp.int32, outgoing)
    slot_ids = lax.iota(jnp.int32, slot_count)
    row_ids = lax.iota(jnp.int32, local_rows)
    routes = []
    for height in range(levels - 1):
        flat_target = target_snode[height].reshape(outgoing)
        owner_dev = flat_target // local_nodes
        target_code = flat_target % local_nodes * row_blocks + target_block[height].reshape(
            outgoing
        )
        earlier = (owner_dev[:, None] == owner_dev[None, :]) & (
            block_order[None, :] < block_order[:, None]
        )
        destination = owner_dev * capacity + jnp.sum(earlier.astype(jnp.int32), axis=1)
        placed = destination[None, :] == slot_ids[:, None]
        source = jnp.max(jnp.where(placed, block_order[None, :], -1), axis=1)
        slot_code = jnp.max(jnp.where(placed, target_code[None, :], -1), axis=1).reshape(
            devices, capacity
        )
        routes.append((destination, source, slot_code))
    residual_list = [right_sides[0]]
    lower_sols = [[]]
    arrivals = [[]]
    for height in range(levels):
        front = 0
        solve_result = jnp.einsum(
            "svw,swr->svr", full_diag[height], residual_list[front], precision=precise
        )
        lower_sols[front].append(solve_result)
        if height + 1 < levels:
            destination, source, slot_code = routes[height]
            update = jnp.einsum(
                "skw,swr->skr",
                off_diagonal[height],
                solve_result.astype(jnp.bfloat16),
                preferred_element_type=jnp.float32,
            )
            update = update.astype(jnp.bfloat16).reshape(outgoing, BR * front_width)
            outbound = jnp.where(
                (source >= 0)[:, None], update[jnp.maximum(source, 0)], jnp.zeros((), jnp.bfloat16)
            )
            outbound = outbound.reshape(devices, capacity, BR * front_width)
            inbound, inbound_code = (
                lax.all_to_all(outbound, "snode", split_axis=0, concat_axis=0, tiled=True),
                lax.all_to_all(slot_code, "snode", split_axis=0, concat_axis=0, tiled=True),
            )
            arrived = inbound_code.reshape(slot_count)
            arrivals[front].append(arrived)
            gather_table = (arrived[None, :] == row_ids[:, None]).astype(jnp.bfloat16)
            summed = jnp.dot(
                gather_table,
                inbound.reshape(slot_count, BR * front_width),
                preferred_element_type=jnp.float32,
            )
            summed = summed.reshape(local_nodes, order_size, front_width)
            upcoming = right_sides[height + 1]
            residual_list[front] = upcoming - summed
    answer = [[None] * levels]
    for height in range(levels - 1, -1, -1):
        front = 0
        if height == levels - 1:
            carried = lower_sols[front][height]
        else:
            destination, source, slot_code = routes[height]
            above_rows = (
                answer[front][height + 1].astype(jnp.bfloat16).reshape(local_rows, BR * front_width)
            )
            arrived = arrivals[front][height]
            outbound = jnp.where(
                (arrived >= 0)[:, None],
                above_rows[jnp.maximum(arrived, 0)],
                jnp.zeros((), jnp.bfloat16),
            )
            outbound = outbound.reshape(devices, capacity, BR * front_width)
            returned = lax.all_to_all(outbound, "snode", split_axis=0, concat_axis=0, tiled=True)
            block_rows = returned.reshape(slot_count, BR * front_width)[destination]
            block_rows = block_rows.reshape(local_nodes, per_node * BR, front_width)
            carried = lower_sols[front][height] - jnp.einsum(
                "skw,skr->swr", off_diagonal[height], block_rows, preferred_element_type=jnp.float32
            )
        result = jnp.einsum("swv,swr->svr", full_diag[height], carried, precision=precise)
        answer[front][height] = result
    stacked = [answer[0][height] for height in range(levels)]
    return jnp.stack(stacked, axis=0)


def solution(mesh):
    in_specs = (
        P(None, "snode", None, "rhs"),
        P(None, "snode", "rhs", None),
        P(None, "snode", None, None),
        P(None, "snode", None),
        P(None, "snode", None),
    )
    out_specs = P(None, "snode", None, "rhs")
    return jax.shard_map(
        on_device, mesh=mesh, in_specs=in_specs, out_specs=out_specs, check_vma=False
    )
```

profile of v0, /device:TPU:41, one launch (start us, length us, event | category | flops | bytes accessed | tf_op | source)
XLA Modules:
  0.0 373.4 jit_solution(11072806632343055890)
XLA Ops:
  2.8 19.3 %all-to-all-start = ((s32[128,1,2]{2,1,0:T(1,128)}), s32[128,1,2]{2,1,0:T(1,128)S(1)}, u32[]{:S(2)}, u32[]{:S(2)}) async-start(s32[128,1,2]{2,1,0:T(1,128)} %bitcast.2), calls=%async_computation | async-start | bytes 131072 | tf_op jit(solution)/shard_map/all_to_all | solution.py:71
  23.9 11.0 %all-gather = f32[1,2,256,256]{3,2,1,0:T(8,128)S(1)} all-gather(f32[1,2,64,256]{3,2,1,0:T(8,128)S(1)} %get-tuple-element.13), channel_id=2, replica_groups=mesh['snode'=128,'rhs'=4] {'rhs'}, dimensions={2}, use_global_device_ids=true | all-gather | bytes 655360 | tf_op jit(solution)/shard_map/all_gather | solution.py:25
  40.5 2.3 gather_fusion
  42.8 1.7 gather.27
  45.5 18.8 %all-to-all-start.2 = ((s32[128,1,2]{2,1,0:T(1,128)}), s32[128,1,2]{2,1,0:T(1,128)S(1)}, u32[]{:S(2)}, u32[]{:S(2)}) async-start(s32[128,1,2]{2,1,0:T(1,128)} %bitcast.8), calls=%async_computation.2 | async-start | bytes 131072 | tf_op jit(solution)/shard_map/all_to_all | solution.py:71
  64.3 2.0 broadcast_select_fusion.2
  66.3 12.2 %all-to-all-done.2 = s32[128,1,2]{2,1,0:T(1,128)S(1)} async-done(((s32[128,1,2]{2,1,0:T(1,128)}), s32[128,1,2]{2,1,0:T(1,128)S(1)}, u32[]{:S(2)}, u32[]{:S(2)}) %all-to-all-start.2) | async-done | bytes 1056 | tf_op jit(solution)/shard_map/all_to_all | solution.py:71
  78.4 7.5 %all-to-all-start.1 = ((bf16[128,2,2048]{2,1,0:T(2,128)(2,1)}), bf16[128,2,2048]{2,1,0:T(2,128)(2,1)}, u32[]{:S(2)}, u32[]{:S(2)}) async-start(bf16[128,2,2048]{2,1,0:T(2,128)(2,1)} %broadcast_select_fusion.2), calls=%async_computation.1 | async-start | bytes 2097152 | tf_op jit(solution)/shard_map/all_to_all | solution.py:70
  86.7 11.3 %all-gather.1 = f32[1,2,256,256]{3,2,1,0:T(8,128)S(1)} all-gather(f32[1,2,64,256]{3,2,1,0:T(8,128)S(1)} %get-tuple-element.15), channel_id=3, replica_groups=mesh['snode'=128,'rhs'=4] {'rhs'}, dimensions={2}, use_global_device_ids=true | all-gather | bytes 655360 | tf_op jit(solution)/shard_map/all_gather | solution.py:25
  98.5 1.9 maximum_reduce_fusion
  100.6 40.6 %all-to-all-done.1 = bf16[128,2,2048]{2,1,0:T(2,128)(2,1)} async-done(((bf16[128,2,2048]{2,1,0:T(2,128)(2,1)}), bf16[128,2,2048]{2,1,0:T(2,128)(2,1)}, u32[]{:S(2)}, u32[]{:S(2)}) %all-to-all-start.1) | async-done | bytes 1048608 | tf_op jit(solution)/shard_map/all_to_all | solution.py:70
  141.2 2.3 reshape.483
  147.7 2.5 gather_fusion.1
  151.9 2.0 broadcast_select_fusion
  154.0 7.0 %all-to-all-start.3 = ((bf16[128,2,2048]{2,1,0:T(2,128)(2,1)}), bf16[128,2,2048]{2,1,0:T(2,128)(2,1)}, u32[]{:S(2)}, u32[]{:S(2)}) async-start(bf16[128,2,2048]{2,1,0:T(2,128)(2,1)} %broadcast_select_fusion), calls=%async_computation.3 | async-start | bytes 2097152 | tf_op jit(solution)/shard_map/all_to_all | solution.py:70
  161.0 11.1 %all-gather.2 = f32[1,2,256,256]{3,2,1,0:T(8,128)S(1)} all-gather(f32[1,2,64,256]{3,2,1,0:T(8,128)S(1)} %copy-done.11), channel_id=4, replica_groups=mesh['snode'=128,'rhs'=4] {'rhs'}, dimensions={2}, use_global_device_ids=true | all-gather | bytes 655360 | tf_op jit(solution)/shard_map/all_gather | solution.py:25
  173.3 42.9 %all-to-all-done.3 = bf16[128,2,2048]{2,1,0:T(2,128)(2,1)} async-done(((bf16[128,2,2048]{2,1,0:T(2,128)(2,1)}), bf16[128,2,2048]{2,1,0:T(2,128)(2,1)}, u32[]{:S(2)}, u32[]{:S(2)}) %all-to-all-start.3) | async-done | bytes 1048608 | tf_op jit(solution)/shard_map/all_to_all | solution.py:70
  216.2 2.3 reshape.486
  226.0 3.3 broadcast_select_fusion.1
  229.3 7.2 %all-to-all-start.4 = ((bf16[128,2,2048]{2,1,0:T(2,128)(2,1)}), bf16[128,2,2048]{2,1,0:T(2,128)(2,1)}, u32[]{:S(2)}, u32[]{:S(2)}) async-start(bf16[128,2,2048]{2,1,0:T(2,128)(2,1)} %broadcast_select_fusion.1), calls=%async_computation.4 | async-start | bytes 2097152 | tf_op jit(solution)/shard_map/all_to_all | solution.py:101
  237.7 54.0 %all-to-all-done.4 = bf16[128,2,2048]{2,1,0:T(2,128)(2,1)} async-done(((bf16[128,2,2048]{2,1,0:T(2,128)(2,1)}), bf16[128,2,2048]{2,1,0:T(2,128)(2,1)}, u32[]{:S(2)}, u32[]{:S(2)}) %all-to-all-start.4) | async-done | bytes 1048608 | tf_op jit(solution)/shard_map/all_to_all | solution.py:101
  301.0 3.2 broadcast_select_fusion.3
  304.2 7.0 %all-to-all-start.5 = ((bf16[128,2,2048]{2,1,0:T(2,128)(2,1)}), bf16[128,2,2048]{2,1,0:T(2,128)(2,1)}, u32[]{:S(2)}, u32[]{:S(2)}) async-start(bf16[128,2,2048]{2,1,0:T(2,128)(2,1)} %broadcast_select_fusion.3), calls=%async_computation.5 | async-start | bytes 2097152 | tf_op jit(solution)/shard_map/all_to_all | solution.py:101
  311.3 55.1 %all-to-all-done.5 = bf16[128,2,2048]{2,1,0:T(2,128)(2,1)} async-done(((bf16[128,2,2048]{2,1,0:T(2,128)(2,1)}), bf16[128,2,2048]{2,1,0:T(2,128)(2,1)}, u32[]{:S(2)}, u32[]{:S(2)}) %all-to-all-start.5) | async-done | bytes 1048608 | tf_op jit(solution)/shard_map/all_to_all | solution.py:101
  (126 shorter events, 44.5 us)
Async XLA Ops:
  0.0 37.5 %copy-start = (bf16[2,2,1024,256]{3,2,1,0:T(8,128)(2,1)S(1)}, bf16[2,2,1024,256]{3,2,1,0:T(8,128)(2,1)}, u32[]{:S(2)}) copy-start(bf16[2,2,1024,256]{3,2,1,0:T(8,128)(2,1)} %param.7) | copy-start | bytes 6291460
  0.9 37.1 %copy-start.17 = (s32[1,2,64]{2,1,0:T(2,128)}, s32[1,2,64]{2,1,0:T(2,128)S(1)}, u32[]{:S(2)}) copy-start(s32[1,2,64]{2,1,0:T(2,128)S(1)} %get-tuple-element.16) | copy-start | bytes 1540
  1.9 22.0 %copy-start.19 = (s32[128]{0:T(128)}, s32[128]{0:T(128)S(1)}, u32[]{:S(2)}) copy-start(s32[128]{0:T(128)S(1)} %convert_reduce_fusion.1) | copy-start | bytes 1540
  2.8 42.6 %all-to-all-start = ((s32[128,1,2]{2,1,0:T(1,128)}), s32[128,1,2]{2,1,0:T(1,128)S(1)}, u32[]{:S(2)}, u32[]{:S(2)}) async-start(s32[128,1,2]{2,1,0:T(1,128)} %bitcast.2), calls=%async_computation | async-start | bytes 131072 | tf_op jit(solution)/shard_map/all_to_all | solution.py:71
  34.9 3.3 copy-start.1
  35.2 5.2 %copy-start.21 = (s32[128]{0:T(128)}, s32[128]{0:T(128)S(1)}, u32[]{:S(2)}) copy-start(s32[128]{0:T(128)S(1)} %convert_reduce_fusion) | copy-start | bytes 1540
  45.5 53.0 %copy-start.9 = (s32[128,1,2]{2,1,0:T(1,128)}, s32[128,1,2]{2,1,0:T(1,128)S(1)}, u32[]{:S(2)}) copy-start(s32[128,1,2]{2,1,0:T(1,128)S(1)} %all-to-all-done) | copy-start | bytes 3076
  45.5 32.9 %all-to-all-start.2 = ((s32[128,1,2]{2,1,0:T(1,128)}), s32[128,1,2]{2,1,0:T(1,128)S(1)}, u32[]{:S(2)}, u32[]{:S(2)}) async-start(s32[128,1,2]{2,1,0:T(1,128)} %bitcast.8), calls=%async_computation.2 | async-start | bytes 131072 | tf_op jit(solution)/shard_map/all_to_all | solution.py:71
  78.4 62.8 %all-to-all-start.1 = ((bf16[128,2,2048]{2,1,0:T(2,128)(2,1)}), bf16[128,2,2048]{2,1,0:T(2,128)(2,1)}, u32[]{:S(2)}, u32[]{:S(2)}) async-start(bf16[128,2,2048]{2,1,0:T(2,128)(2,1)} %broadcast_select_fusion.2), calls=%async_computation.1 | async-start | bytes 2097152 | tf_op jit(solution)/shard_map/all_to_all | solution.py:70
  98.0 47.1 %copy-start.3 = (f32[1,2,256,256]{3,2,1,0:T(8,128)}, f32[1,2,256,256]{3,2,1,0:T(8,128)S(1)}, u32[]{:S(2)}) copy-start(f32[1,2,256,256]{3,2,1,0:T(8,128)S(1)} %all-gather.1) | copy-start | bytes 1572868
  151.9 20.3 %copy-start.13 = (s32[128,2]{1,0:T(8,128)S(1)}, s32[128,2]{1,0:T(8,128)}, u32[]{:S(2)}) copy-start(s32[128,2]{1,0:T(8,128)} %get-tuple-element.29) | copy-start | bytes 3076
  154.0 7.0 %copy-start.11 = (f32[1,2,64,256]{3,2,1,0:T(8,128)S(1)}, f32[1,2,64,256]{3,2,1,0:T(8,128)}, u32[]{:S(2)}) copy-start(f32[1,2,64,256]{3,2,1,0:T(8,128)} %get-tuple-element.14) | copy-start | bytes 393220
  154.0 18.1 %copy-start.14 = (s32[128,2]{1,0:T(8,128)S(1)}, s32[128,2]{1,0:T(8,128)}, u32[]{:S(2)}) copy-start(s32[128,2]{1,0:T(8,128)} %get-tuple-element.28) | copy-start | bytes 3076
  154.0 62.2 %all-to-all-start.3 = ((bf16[128,2,2048]{2,1,0:T(2,128)(2,1)}), bf16[128,2,2048]{2,1,0:T(2,128)(2,1)}, u32[]{:S(2)}, u32[]{:S(2)}) async-start(bf16[128,2,2048]{2,1,0:T(2,128)(2,1)} %broadcast_select_fusion), calls=%async_computation.3 | async-start | bytes 2097152 | tf_op jit(solution)/shard_map/all_to_all | solution.py:70
  226.0 10.5 %copy-start.18 = (s32[1,2,64]{2,1,0:T(2,128)S(1)}, s32[1,2,64]{2,1,0:T(2,128)}, u32[]{:S(2)}) copy-start(s32[1,2,64]{2,1,0:T(2,128)} %copy-done.17) | copy-start | bytes 1540
  226.0 10.5 %copy-start.22 = (s32[128]{0:T(128)S(1)}, s32[128]{0:T(128)}, u32[]{:S(2)}) copy-start(s32[128]{0:T(128)} %copy-done.21) | copy-start | bytes 1540
  226.0 10.6 %copy-start.12 = (s32[128,2]{1,0:T(8,128)S(1)}, s32[128,2]{1,0:T(8,128)}, u32[]{:S(2)}) copy-start(s32[128,2]{1,0:T(8,128)} %get-tuple-element.5) | copy-start | bytes 3076
  226.0 10.7 %copy-start.10 = (s32[128,1,2]{2,1,0:T(1,128)S(1)}, s32[128,1,2]{2,1,0:T(1,128)}, u32[]{:S(2)}) copy-start(s32[128,1,2]{2,1,0:T(1,128)} %copy-done.9) | copy-start | bytes 3076
  229.3 62.4 %all-to-all-start.4 = ((bf16[128,2,2048]{2,1,0:T(2,128)(2,1)}), bf16[128,2,2048]{2,1,0:T(2,128)(2,1)}, u32[]{:S(2)}, u32[]{:S(2)}) async-start(bf16[128,2,2048]{2,1,0:T(2,128)(2,1)} %broadcast_select_fusion.1), calls=%async_computation.4 | async-start | bytes 2097152 | tf_op jit(solution)/shard_map/all_to_all | solution.py:101
  301.0 10.2 %copy-start.16 = (s32[1,2,64]{2,1,0:T(2,128)S(1)}, s32[1,2,64]{2,1,0:T(2,128)}, u32[]{:S(2)}) copy-start(s32[1,2,64]{2,1,0:T(2,128)} %copy-done.15) | copy-start | bytes 1540
  301.0 10.3 %copy-start.20 = (s32[128]{0:T(128)S(1)}, s32[128]{0:T(128)}, u32[]{:S(2)}) copy-start(s32[128]{0:T(128)} %copy-done.19) | copy-start | bytes 1540
  304.2 62.2 %all-to-all-start.5 = ((bf16[128,2,2048]{2,1,0:T(2,128)(2,1)}), bf16[128,2,2048]{2,1,0:T(2,128)(2,1)}, u32[]{:S(2)}, u32[]{:S(2)}) async-start(bf16[128,2,2048]{2,1,0:T(2,128)(2,1)} %broadcast_select_fusion.3), calls=%async_computation.5 | async-start | bytes 2097152 | tf_op jit(solution)/shard_map/all_to_all | solution.py:101
  367.8 3.1 copy-start.6
  369.6 1.9 copy-start.2
  (5 other events, 5.9 us)
where the time goes:
time: 374 us; the launch traced here: 373 us
  waiting for transfers between devices  205 us (55%)
  starting transfers between devices  66.6 us (18%)
  local copies, waits for them, and re-layouts  40.2 us (11%)
  blocking collectives  33.4 us (9%)
  other arithmetic  15.2 us (4%)
  matrix products  12.6 us (3%)
    all_to_all x4, waiting for transfers between devices, on_device(): lax.all_to_all(outbound, 'snode', split_axis=0, concat_axis=0, tiled=True)  193 us
    all_to_all x2, starting transfers between devices, on_device(): lax.all_to_all(slot_code, 'snode', split_axis=0, concat_axis=0, tiled=True)  38 us
    all_gather x3, blocking collectives, on_device(): lax.all_gather(diag_inverse[height], 'rhs', axis=1, tiled=True)  33.4 us
    all_to_all x4, starting transfers between devices, on_device(): lax.all_to_all(outbound, 'snode', split_axis=0, concat_axis=0, tiled=True)  28.6 us
    all_to_all x2, waiting for transfers between devices, on_device(): lax.all_to_all(slot_code, 'snode', split_axis=0, concat_axis=0, tiled=True)  12.2 us
    gather x4, local copies, waits for them, and re-layouts, on_device(): update[jnp.maximum(source, 0)]  8.3 us
  transfers between devices with their start and end apart: 6, of which 5 were waited for; matrix products, arithmetic and copies ran while one was open for 5% of the time, Pallas kernels for 0%

commit v1 on v0

--- a/solution.py
+++ b/solution.py
@@ -22,7 +22,11 @@
     front_count = 1
     front_width = columns // front_count
     full_diag = [
-        lax.all_gather(diag_inverse[height], "rhs", axis=1, tiled=True) for height in range(levels)
+        jnp.concatenate(
+            lax.all_to_all(jnp.stack([diag_inverse[height]] * lax.axis_size("rhs")), "rhs", 0, 0),
+            axis=1,
+        )
+        for height in range(levels)
     ]
     block_order = lax.iota(jnp.int32, outgoing)
     slot_ids = lax.iota(jnp.int32, slot_count)

time: 374 us -> 387 us (1.035)
  waiting for transfers between devices: 205 us -> 243 us
  blocking collectives: 33.4 us -> 0 us
  starting transfers between devices: 66.6 us -> 72 us
    all_gather x3 -> x0, blocking collectives: 33.4 us -> none  [on_device(): lax.all_gather(diag_inverse[height], 'rhs', axis=1, tiled=True)]
    all_to_all x4, waiting for transfers between devices: 193 us -> 213 us  [on_device(): lax.all_to_all(outbound, 'snode', split_axis=0, concat_axis=0, tiled=True)]
    all_to_all x0 -> x3, starting transfers between devices: none -> 15.1 us  [on_device(): lax.all_to_all(jnp.stack([diag_inverse[height]] * lax.axis_size('rhs')),...]
    all_to_all x2, starting transfers between devices: 38 us -> 27 us  [on_device(): lax.all_to_all(slot_code, 'snode', split_axis=0, concat_axis=0, tiled=True)]
    all_to_all x2, waiting for transfers between devices: 12.2 us -> 20.8 us  [on_device(): lax.all_to_all(slot_code, 'snode', split_axis=0, concat_axis=0, tiled=True)]
    all_to_all x0 -> x3, waiting for transfers between devices: none -> 8.3 us  [on_device(): lax.all_to_all(jnp.stack([diag_inverse[height]] * lax.axis_size('rhs')),...]
  transfers between devices with their start and end apart: 6 -> 9, of which waited for: 5 -> 8; matrix products, arithmetic and copies ran while one was open for 5% -> 8% of each run, Pallas kernels for 0% -> 0%
where the time goes in v1:
time: 387 us; the launch traced here: 386 us
  waiting for transfers between devices  243 us (63%)
  starting transfers between devices  72 us (19%)
  local copies, waits for them, and re-layouts  42.7 us (11%)
  other arithmetic  15.6 us (4%)
  matrix products  12.7 us (3%)
    all_to_all x4, waiting for transfers between devices, on_device(): lax.all_to_all(outbound, 'snode', split_axis=0, concat_axis=0, tiled=True)  213 us
    all_to_all x4, starting transfers between devices, on_device(): lax.all_to_all(outbound, 'snode', split_axis=0, concat_axis=0, tiled=True)  29.9 us
    all_to_all x2, starting transfers between devices, on_device(): lax.all_to_all(slot_code, 'snode', split_axis=0, concat_axis=0, tiled=True)  27 us
    all_to_all x2, waiting for transfers between devices, on_device(): lax.all_to_all(slot_code, 'snode', split_axis=0, concat_axis=0, tiled=True)  20.8 us
    all_to_all x3, starting transfers between devices, on_device(): lax.all_to_all(jnp.stack([diag_inverse[height]] * lax.axis_size('rhs')),...  15.1 us
    gather x4, local copies, waits for them, and re-layouts, on_device(): update[jnp.maximum(source, 0)]  8.41 us
    all_to_all x3, waiting for transfers between devices, on_device(): lax.all_to_all(jnp.stack([diag_inverse[height]] * lax.axis_size('rhs')),...  8.3 us
  transfers between devices with their start and end apart: 9, of which 8 were waited for; matrix products, arithmetic and copies ran while one was open for 8% of the time, Pallas kernels for 0%

profile of v1, /device:TPU:41, one launch (start us, length us, event | category | flops | bytes accessed | tf_op | source)
XLA Modules:
  0.0 386.1 jit_solution(8707590542152738874)
XLA Ops:
  2.6 4.3 %all-to-all-start = ((f32[4,2,64,256]{3,2,1,0:T(8,128)}), f32[4,2,64,256]{3,2,1,0:T(8,128)S(1)}, u32[]{:S(2)}, u32[]{:S(2)}) async-start(f32[4,2,64,256]{3,2,1,0:T(8,128)} %stack.21), calls=%async_computation | async-start | bytes 1048576 | tf_op jit(solution)/shard_map/all_to_all | solution.py:26
  11.8 2.3 all-to-all-done
  14.1 20.7 %all-to-all-start.1 = ((s32[128,1,2]{2,1,0:T(1,128)}), s32[128,1,2]{2,1,0:T(1,128)S(1)}, u32[]{:S(2)}, u32[]{:S(2)}) async-start(s32[128,1,2]{2,1,0:T(1,128)} %bitcast.4), calls=%async_computation.1 | async-start | bytes 131072 | tf_op jit(solution)/shard_map/all_to_all | solution.py:75
  37.3 11.8 %all-to-all-done.1 = s32[128,1,2]{2,1,0:T(1,128)S(1)} async-done(((s32[128,1,2]{2,1,0:T(1,128)}), s32[128,1,2]{2,1,0:T(1,128)S(1)}, u32[]{:S(2)}, u32[]{:S(2)}) %all-to-all-start.1) | async-done | bytes 1056 | tf_op jit(solution)/shard_map/all_to_all | solution.py:75
  49.1 6.3 %all-to-all-start.4 = ((s32[128,1,2]{2,1,0:T(1,128)}), s32[128,1,2]{2,1,0:T(1,128)S(1)}, u32[]{:S(2)}, u32[]{:S(2)}) async-start(s32[128,1,2]{2,1,0:T(1,128)} %bitcast.12), calls=%async_computation.4 | async-start | bytes 131072 | tf_op jit(solution)/shard_map/all_to_all | solution.py:75
  56.5 2.5 gather_fusion
  60.8 9.0 %all-to-all-done.4 = s32[128,1,2]{2,1,0:T(1,128)S(1)} async-done(((s32[128,1,2]{2,1,0:T(1,128)}), s32[128,1,2]{2,1,0:T(1,128)S(1)}, u32[]{:S(2)}, u32[]{:S(2)}) %all-to-all-start.4) | async-done | bytes 1056 | tf_op jit(solution)/shard_map/all_to_all | solution.py:75
  70.6 5.3 %all-to-all-start.3 = ((f32[4,2,64,256]{3,2,1,0:T(8,128)}), f32[4,2,64,256]{3,2,1,0:T(8,128)}, u32[]{:S(2)}, u32[]{:S(2)}) async-start(f32[4,2,64,256]{3,2,1,0:T(8,128)} %stack.22), calls=%async_computation.3 | async-start | bytes 1048576 | tf_op jit(solution)/shard_map/all_to_all | solution.py:26
  77.9 6.0 %all-to-all-done.3 = f32[4,2,64,256]{3,2,1,0:T(8,128)} async-done(((f32[4,2,64,256]{3,2,1,0:T(8,128)}), f32[4,2,64,256]{3,2,1,0:T(8,128)}, u32[]{:S(2)}, u32[]{:S(2)}) %all-to-all-start.3) | async-done | bytes 524320 | tf_op jit(solution)/shard_map/all_to_all | solution.py:26
  83.9 8.6 %all-to-all-start.2 = ((bf16[128,2,2048]{2,1,0:T(2,128)(2,1)}), bf16[128,2,2048]{2,1,0:T(2,128)(2,1)}, u32[]{:S(2)}, u32[]{:S(2)}) async-start(bf16[128,2,2048]{2,1,0:T(2,128)(2,1)} %broadcast_select_fusion.2), calls=%async_computation.2 | async-start | bytes 2097152 | tf_op jit(solution)/shard_map/all_to_all | solution.py:74
  96.4 51.4 %all-to-all-done.2 = bf16[128,2,2048]{2,1,0:T(2,128)(2,1)} async-done(((bf16[128,2,2048]{2,1,0:T(2,128)(2,1)}), bf16[128,2,2048]{2,1,0:T(2,128)(2,1)}, u32[]{:S(2)}, u32[]{:S(2)}) %all-to-all-start.2) | async-done | bytes 1048608 | tf_op jit(solution)/shard_map/all_to_all | solution.py:74
  148.6 5.5 %all-to-all-start.6 = ((f32[4,2,64,256]{3,2,1,0:T(8,128)}), f32[4,2,64,256]{3,2,1,0:T(8,128)}, u32[]{:S(2)}, u32[]{:S(2)}) async-start(f32[4,2,64,256]{3,2,1,0:T(8,128)} %stack.23), calls=%async_computation.6 | async-start | bytes 1048576 | tf_op jit(solution)/shard_map/all_to_all | solution.py:26
  154.0 2.2 reshape.506
  160.5 2.4 gather_fusion.1
  164.7 2.0 broadcast_select_fusion
  166.7 7.4 %all-to-all-start.5 = ((bf16[128,2,2048]{2,1,0:T(2,128)(2,1)}), bf16[128,2,2048]{2,1,0:T(2,128)(2,1)}, u32[]{:S(2)}, u32[]{:S(2)}) async-start(bf16[128,2,2048]{2,1,0:T(2,128)(2,1)} %broadcast_select_fusion), calls=%async_computation.5 | async-start | bytes 2097152 | tf_op jit(solution)/shard_map/all_to_all | solution.py:74
  176.3 52.9 %all-to-all-done.5 = bf16[128,2,2048]{2,1,0:T(2,128)(2,1)} async-done(((bf16[128,2,2048]{2,1,0:T(2,128)(2,1)}), bf16[128,2,2048]{2,1,0:T(2,128)(2,1)}, u32[]{:S(2)}, u32[]{:S(2)}) %all-to-all-start.5) | async-done | bytes 1048608 | tf_op jit(solution)/shard_map/all_to_all | solution.py:74
  229.2 2.2 reshape.511
  239.1 3.2 broadcast_select_fusion.1
  242.3 7.0 %all-to-all-start.7 = ((bf16[128,2,2048]{2,1,0:T(2,128)(2,1)}), bf16[128,2,2048]{2,1,0:T(2,128)(2,1)}, u32[]{:S(2)}, u32[]{:S(2)}) async-start(bf16[128,2,2048]{2,1,0:T(2,128)(2,1)} %broadcast_select_fusion.1), calls=%async_computation.7 | async-start | bytes 2097152 | tf_op jit(solution)/shard_map/all_to_all | solution.py:105
  250.5 54.0 %all-to-all-done.7 = bf16[128,2,2048]{2,1,0:T(2,128)(2,1)} async-done(((bf16[128,2,2048]{2,1,0:T(2,128)(2,1)}), bf16[128,2,2048]{2,1,0:T(2,128)(2,1)}, u32[]{:S(2)}, u32[]{:S(2)}) %all-to-all-start.7) | async-done | bytes 1048608 | tf_op jit(solution)/shard_map/all_to_all | solution.py:105
  313.8 3.2 broadcast_select_fusion.3
  317.0 7.0 %all-to-all-start.8 = ((bf16[128,2,2048]{2,1,0:T(2,128)(2,1)}), bf16[128,2,2048]{2,1,0:T(2,128)(2,1)}, u32[]{:S(2)}, u32[]{:S(2)}) async-start(bf16[128,2,2048]{2,1,0:T(2,128)(2,1)} %broadcast_select_fusion.3), calls=%async_computation.8 | async-start | bytes 2097152 | tf_op jit(solution)/shard_map/all_to_all | solution.py:105
  324.0 55.1 %all-to-all-done.8 = bf16[128,2,2048]{2,1,0:T(2,128)(2,1)} async-done(((bf16[128,2,2048]{2,1,0:T(2,128)(2,1)}), bf16[128,2,2048]{2,1,0:T(2,128)(2,1)}, u32[]{:S(2)}, u32[]{:S(2)}) %all-to-all-start.8) | async-done | bytes 1048608 | tf_op jit(solution)/shard_map/all_to_all | solution.py:105
  (145 shorter events, 53.2 us)
Async XLA Ops:
  1.8 53.7 %copy-start = (bf16[2,2,1024,256]{3,2,1,0:T(8,128)(2,1)S(1)}, bf16[2,2,1024,256]{3,2,1,0:T(8,128)(2,1)}, u32[]{:S(2)}) copy-start(bf16[2,2,1024,256]{3,2,1,0:T(8,128)(2,1)} %param.7) | copy-start | bytes 6291460
  2.6 11.5 %all-to-all-start = ((f32[4,2,64,256]{3,2,1,0:T(8,128)}), f32[4,2,64,256]{3,2,1,0:T(8,128)S(1)}, u32[]{:S(2)}, u32[]{:S(2)}) async-start(f32[4,2,64,256]{3,2,1,0:T(8,128)} %stack.21), calls=%async_computation | async-start | bytes 1048576 | tf_op jit(solution)/shard_map/all_to_all | solution.py:26
  7.0 42.1 %copy-start.22 = (s32[1,2,64]{2,1,0:T(2,128)}, s32[1,2,64]{2,1,0:T(2,128)S(1)}, u32[]{:S(2)}) copy-start(s32[1,2,64]{2,1,0:T(2,128)S(1)} %get-tuple-element.16) | copy-start | bytes 1540
  14.1 35.0 %all-to-all-start.1 = ((s32[128,1,2]{2,1,0:T(1,128)}), s32[128,1,2]{2,1,0:T(1,128)S(1)}, u32[]{:S(2)}, u32[]{:S(2)}) async-start(s32[128,1,2]{2,1,0:T(1,128)} %bitcast.4), calls=%async_computation.1 | async-start | bytes 131072 | tf_op jit(solution)/shard_map/all_to_all | solution.py:75
  37.3 18.7 %copy-start.5 = (f32[2,256,128]{2,1,0:T(8,128)}, f32[2,256,128]{2,1,0:T(8,128)S(1)}, u32[]{:S(2)}) copy-start(f32[2,256,128]{2,1,0:T(8,128)S(1)} %fusion.13) | copy-start | bytes 786436
  49.1 44.1 %copy-start.9 = (s32[128,1,2]{2,1,0:T(1,128)}, s32[128,1,2]{2,1,0:T(1,128)S(1)}, u32[]{:S(2)}) copy-start(s32[128,1,2]{2,1,0:T(1,128)S(1)} %all-to-all-done.1) | copy-start | bytes 3076
  49.1 20.7 %all-to-all-start.4 = ((s32[128,1,2]{2,1,0:T(1,128)}), s32[128,1,2]{2,1,0:T(1,128)S(1)}, u32[]{:S(2)}, u32[]{:S(2)}) async-start(s32[128,1,2]{2,1,0:T(1,128)} %bitcast.12), calls=%async_computation.4 | async-start | bytes 131072 | tf_op jit(solution)/shard_map/all_to_all | solution.py:75
  59.0 10.8 %copy-start.14 = (f32[2,64,256]{2,1,0:T(8,128)S(1)}, f32[2,64,256]{2,1,0:T(8,128)}, u32[]{:S(2)}) copy-start(f32[2,64,256]{2,1,0:T(8,128)} %get-tuple-element.15) | copy-start | bytes 393220
  69.8 23.5 %copy-start.11 = (s32[128,1,2]{2,1,0:T(1,128)}, s32[128,1,2]{2,1,0:T(1,128)S(1)}, u32[]{:S(2)}) copy-start(s32[128,1,2]{2,1,0:T(1,128)S(1)} %all-to-all-done.4) | copy-start | bytes 3076
  70.6 13.3 %all-to-all-start.3 = ((f32[4,2,64,256]{3,2,1,0:T(8,128)}), f32[4,2,64,256]{3,2,1,0:T(8,128)}, u32[]{:S(2)}, u32[]{:S(2)}) async-start(f32[4,2,64,256]{3,2,1,0:T(8,128)} %stack.22), calls=%async_computation.3 | async-start | bytes 1048576 | tf_op jit(solution)/shard_map/all_to_all | solution.py:26
  75.9 16.6 %copy-start.17 = (s32[256]{0:T(256)S(1)}, s32[256]{0:T(256)}, u32[]{:S(2)}) copy-start(s32[256]{0:T(256)} %get-tuple-element.10) | copy-start | bytes 3076
  77.9 69.9 %copy-start.13 = (f32[2,64,256]{2,1,0:T(8,128)S(1)}, f32[2,64,256]{2,1,0:T(8,128)}, u32[]{:S(2)}) copy-start(f32[2,64,256]{2,1,0:T(8,128)} %get-tuple-element.14) | copy-start | bytes 393220
  83.9 63.9 %all-to-all-start.2 = ((bf16[128,2,2048]{2,1,0:T(2,128)(2,1)}), bf16[128,2,2048]{2,1,0:T(2,128)(2,1)}, u32[]{:S(2)}, u32[]{:S(2)}) async-start(bf16[128,2,2048]{2,1,0:T(2,128)(2,1)} %broadcast_select_fusion.2), calls=%async_computation.2 | async-start | bytes 2097152 | tf_op jit(solution)/shard_map/all_to_all | solution.py:74
  96.3 61.5 %copy-start.3 = (f32[2,4,64,256]{3,2,1,0:T(8,128)}, f32[2,4,64,256]{3,2,1,0:T(8,128)S(1)}, u32[]{:S(2)}) copy-start(f32[2,4,64,256]{3,2,1,0:T(8,128)S(1)} %copy.62) | copy-start | bytes 1572868
  148.6 18.1 %all-to-all-start.6 = ((f32[4,2,64,256]{3,2,1,0:T(8,128)}), f32[4,2,64,256]{3,2,1,0:T(8,128)}, u32[]{:S(2)}, u32[]{:S(2)}) async-start(f32[4,2,64,256]{3,2,1,0:T(8,128)} %stack.23), calls=%async_computation.6 | async-start | bytes 1048576 | tf_op jit(solution)/shard_map/all_to_all | solution.py:26
  166.7 62.6 %all-to-all-start.5 = ((bf16[128,2,2048]{2,1,0:T(2,128)(2,1)}), bf16[128,2,2048]{2,1,0:T(2,128)(2,1)}, u32[]{:S(2)}, u32[]{:S(2)}) async-start(bf16[128,2,2048]{2,1,0:T(2,128)(2,1)} %broadcast_select_fusion), calls=%async_computation.5 | async-start | bytes 2097152 | tf_op jit(solution)/shard_map/all_to_all | solution.py:74
  239.1 10.2 %copy-start.23 = (s32[1,2,64]{2,1,0:T(2,128)S(1)}, s32[1,2,64]{2,1,0:T(2,128)}, u32[]{:S(2)}) copy-start(s32[1,2,64]{2,1,0:T(2,128)} %copy-done.22) | copy-start | bytes 1540
  239.1 10.3 %copy-start.27 = (s32[128]{0:T(128)S(1)}, s32[128]{0:T(128)}, u32[]{:S(2)}) copy-start(s32[128]{0:T(128)} %copy-done.26) | copy-start | bytes 1540
  239.1 10.3 %copy-start.15 = (s32[128,2]{1,0:T(8,128)S(1)}, s32[128,2]{1,0:T(8,128)}, u32[]{:S(2)}) copy-start(s32[128,2]{1,0:T(8,128)} %get-tuple-element.5) | copy-start | bytes 3076
  239.1 10.5 %copy-start.10 = (s32[128,1,2]{2,1,0:T(1,128)S(1)}, s32[128,1,2]{2,1,0:T(1,128)}, u32[]{:S(2)}) copy-start(s32[128,1,2]{2,1,0:T(1,128)} %copy-done.9) | copy-start | bytes 3076
  242.3 62.2 %all-to-all-start.7 = ((bf16[128,2,2048]{2,1,0:T(2,128)(2,1)}), bf16[128,2,2048]{2,1,0:T(2,128)(2,1)}, u32[]{:S(2)}, u32[]{:S(2)}) async-start(bf16[128,2,2048]{2,1,0:T(2,128)(2,1)} %broadcast_select_fusion.1), calls=%async_computation.7 | async-start | bytes 2097152 | tf_op jit(solution)/shard_map/all_to_all | solution.py:105
  313.8 10.2 %copy-start.21 = (s32[1,2,64]{2,1,0:T(2,128)S(1)}, s32[1,2,64]{2,1,0:T(2,128)}, u32[]{:S(2)}) copy-start(s32[1,2,64]{2,1,0:T(2,128)} %copy-done.20) | copy-start | bytes 1540
  313.8 10.3 %copy-start.25 = (s32[128]{0:T(128)S(1)}, s32[128]{0:T(128)}, u32[]{:S(2)}) copy-start(s32[128]{0:T(128)} %copy-done.24) | copy-start | bytes 1540
  317.0 62.2 %all-to-all-start.8 = ((bf16[128,2,2048]{2,1,0:T(2,128)(2,1)}), bf16[128,2,2048]{2,1,0:T(2,128)(2,1)}, u32[]{:S(2)}, u32[]{:S(2)}) async-start(bf16[128,2,2048]{2,1,0:T(2,128)(2,1)} %broadcast_select_fusion.3), calls=%async_computation.8 | async-start | bytes 2097152 | tf_op jit(solution)/shard_map/all_to_all | solution.py:105
  (13 other events, 42.7 us)
